TPU v7x, 512 devices: a whole 4x4x16 slice. The times are simulated.
512 devices in a mesh: leaf: 256 (over x, z, y), cols: 2 (over core).
Axes of the slice: x: 4, y: 4, z: 16, core: 2. Of those that a mesh axis runs over, the one named last changes fastest.
Arguments:
- vectors: bfloat16 [128, 524288], P('cols', 'leaf'), may hold values from -6 to 6
- near_blocks: bfloat16 [2048, 8, 256, 256], P('leaf', None, 'cols'), may hold values from -0.125 to 0.125
- near_index: int32 [2048, 8], P('leaf'), may hold values from -1 to 2047, as said below
- far_index: int32 [2048, 8], P('leaf'), may hold values from -1 to 2047, as said below
- far_kind: int32 [2048, 8], P('leaf'), may hold values from 0 to 15
- cluster_basis: bfloat16 [2048, 64, 256], P('leaf'), may hold values from -0.375 to 0.375
- leaf_transfer: float32 [2048, 64, 64], P('leaf'), may hold values from -0.25 to 0.25
- coupling_table: float32 [16, 64, 64], replicated, may hold values from -0.5 to 0.5
- parent_transfer_matrices: float32 [2, 64, 64], replicated, may hold values from -0.625 to 0.625
- coarse_kind: int32 [255], replicated, may hold values from 0 to 15
Outputs:
- product: bfloat16 [128, 524288], P('cols', 'leaf')
Inputs may be any that keep to these rules, and one draw needn't show every extreme that they name: `near_index`: row i holds distinct leaves within 8 positions of leaf i, and -1 in unused slots; its first entry is i itself, its second is i - 8 for even i and i + 8 for odd i, or -1 where that is outside the leaves. No leaf stands in both near_index and far_index of one row. `far_index`: row i holds distinct leaves other than i within 8 positions of leaf i, and -1 in unused slots.
All inputs are finite; a program needn't handle non-finite values.
Results may differ from a plain program's by a relative error of at most 0.0044.
Values may be sent and summed in bfloat16 or wider, within the bound.
No kernel may reach another device: no remote copies, remote signals or barrier semaphores. Data moves between devices by JAX's collectives and lax.ppermute only.
A program may use at most 128 MiB of HBM per device.

v0:
```python
import jax
import jax.numpy as jnp
from jax import lax
from jax.experimental import pallas as pl
from jax.experimental.pallas import tpu as pltpu
from jax.sharding import PartitionSpec as P


F32 = jnp.float32
BF16 = jnp.bfloat16
NT = (((1,), (1,)), ((), ()))


def halves(value):
    high = value.astype(BF16)
    return high, (value - high.astype(F32)).astype(BF16)


def triple_left(value):
    high, low = halves(value)
    return jnp.concatenate([high, low, high], axis=1)


def triple_right(value):
    high, low = halves(value)
    return jnp.concatenate([high, high, low], axis=0)


def dot(left, right):
    return jnp.dot(left, right, preferred_element_type=F32)


def dot_nt(left, right):
    return lax.dot_general(left, right, NT, preferred_element_type=F32)


def fold(value, rank):
    return value[:, :rank] + value[:, rank : 2 * rank]


def lanes(value):
    part = value.shape[0] // 2
    return jnp.concatenate([value[:part], value[part:]], axis=1)


def unlanes(value):
    rank = value.shape[1] // 2
    return jnp.concatenate([value[:, :rank], value[:, rank:]], axis=0)


def bring(sources, targets, arrived):
    copies = [
        pltpu.make_async_copy(source, target, arrived.at[n])
        for n, (source, target) in enumerate(zip(sources, targets))
    ]
    for copy in copies:
        copy.start()
    return copies


def coef_kernel(
    x_hbm, basis_hbm, transfer_hbm, packed_ref, group_ref, x_ref, basis_ref, transfer_ref, arrived
):
    leaves, rank, rows = basis_ref.shape
    for copy in bring(
        (x_hbm, basis_hbm, transfer_hbm), (x_ref, basis_ref, transfer_ref), arrived
    ):
        copy.wait()
    total = jnp.zeros((x_ref.shape[0], rank), F32)
    for i in range(leaves):
        coef = dot_nt(x_ref[:, i * rows : (i + 1) * rows], basis_ref[i])
        start = leaves * rows + i * 2 * rank
        high, low = halves(coef)
        both = jnp.concatenate([high, low], axis=1)
        packed_ref[:, start : start + 2 * rank] = both
        above, below = halves(transfer_ref[i])
        total += dot_nt(both, jnp.concatenate([above, above], axis=1)) + dot_nt(high, below)
    sent = lanes(total.astype(BF16))
    for j in range(group_ref.shape[0]):
        group_ref[j] = sent
    packed_ref[:, : leaves * rows] = x_ref[...]


def path_blocks(g, groups, first, last, down, kind_ref, table_ref, parent_ref, with_sum):
    rank = table_ref.shape[1]
    steps = [triple_left(parent_ref[0]), triple_left(parent_ref[1])]
    across = []
    for level in range(first, last):
        heap = (groups >> (level + 1)) + (g >> (level + 1))
        coupling = table_ref[kind_ref[heap - 1]]
        bit = (g >> level) & 1
        coupling = jnp.where(bit == 1, coupling, coupling.T)
        step = jnp.where(bit == 1, parent_ref[1], parent_ref[0])
        if down is None:
            across.append(coupling)
            down = step
        else:
            right = triple_right(down)
            made = dot(triple_left(jnp.concatenate([coupling, step], axis=0)), right)
            across.append(made[:rank])
            down = made[rank:]
    upward = jnp.concatenate([parent_ref[0].T, parent_ref[1].T], axis=0)
    left = triple_left(upward)
    trees = [[block] for block in across]
    if with_sum:
        trees.append([upward[:rank], upward[rank:]])
    for step in range(1, last - first):
        live = [t for t in range(len(trees)) if t >= step]
        blocks = [block for t in live for block in trees[t]]
        made = dot(left, triple_right(jnp.concatenate(blocks, axis=1)))
        at = 0
        for t in live:
            grown = []
            for _ in trees[t]:
                for b in range(2):
                    grown.append(made[b * rank : (b + 1) * rank, at * rank : (at + 1) * rank])
                at += 1
            trees[t] = grown
    return trees, down


def store_blocks(trees, here, ref):
    rank = ref.shape[1]
    ref[here] = jnp.zeros((rank, ref.shape[2]), BF16)
    for t, blocks in enumerate(trees):
        base = ((here >> t) ^ 1) << t
        for v, block in enumerate(blocks):
            ref[base + v, :, : 2 * rank] = jnp.concatenate(halves(block), axis=1)


def low_path_kernel(
    kind_hbm, table_hbm, parent_hbm, low_ref, down_ref, kind_ref, table_ref, parent_ref, arrived
):
    for copy in bring(
        (kind_hbm, table_hbm, parent_hbm), (kind_ref, table_ref, parent_ref), arrived
    ):
        copy.wait()
    g = lax.axis_index("leaf")
    groups = kind_ref.shape[0] + 1
    half = (groups.bit_length() - 1) // 2
    rank = table_ref.shape[1]
    trees, down = path_blocks(
        g, groups, 0, half, None, kind_ref, table_ref, parent_ref, True
    )
    down_ref[...] = down
    store_blocks(trees[:half], g & ((1 << half) - 1), low_ref)
    for j, block in enumerate(trees[half]):
        low_ref[j, :, 2 * rank :] = jnp.concatenate(halves(block), axis=1)


def high_path_kernel(
    kind_hbm, table_hbm, parent_hbm, transfer_hbm, down_ref, high_ref, far_ref, spread_ref,
    kind_ref, table_ref, parent_ref, transfer_ref, arrived,
):
    for copy in bring(
        (kind_hbm, table_hbm, parent_hbm, transfer_hbm),
        (kind_ref, table_ref, parent_ref, transfer_ref),
        arrived,
    ):
        copy.wait()
    g = lax.axis_index("leaf")
    groups = kind_ref.shape[0] + 1
    depth = groups.bit_length() - 1
    half = depth // 2
    rank = table_ref.shape[1]
    for kind in range(table_ref.shape[0]):
        high, low = halves(table_ref[kind])
        far_ref[kind, :rank, :] = jnp.concatenate([high, high], axis=1)
        far_ref[kind, rank:, :] = jnp.concatenate([low, jnp.zeros_like(low)], axis=1)
    for i in range(transfer_ref.shape[0]):
        spread_ref[i] = triple_right(transfer_ref[i])
    trees, _ = path_blocks(
        g, groups, half, depth, down_ref[...], kind_ref, table_ref, parent_ref, False
    )
    store_blocks(trees, g >> half, high_ref)


def middle_kernel(seen_ref, low_ref, own_ref, sent_ref):
    count = seen_ref.shape[0]
    rank = low_ref.shape[1]
    total = dot(unlanes(seen_ref[0]), low_ref[0])
    for j in range(1, count):
        total += dot(unlanes(seen_ref[j]), low_ref[j])
    own_ref[...] = fold(total[:, : 2 * rank], rank)
    sent = lanes(fold(total[:, 2 * rank :], rank).astype(BF16))
    for j in range(count):
        sent_ref[j] = sent


def near_kernel(
    near_hbm, far_index_hbm, far_kind_hbm,
    before_ref, packed_ref, after_ref, own_ref, other_ref, table_ref,
    near_out_ref, far_out_ref, window, coefs, blocks, arrived,
    near_ref, far_index_ref, far_kind_ref, lists_arrived,
):
    lists = bring(
        (near_hbm, far_index_hbm, far_kind_hbm), (near_ref, far_index_ref, far_kind_ref),
        lists_arrived,
    )
    leaves, slots, half, rows = own_ref.shape
    cols = packed_ref.shape[0]
    rank = far_out_ref.shape[2]
    start = (lax.axis_index("leaf") - 1) * leaves
    core = lax.axis_index("cols")

    def fetch(i, side):
        ref = (own_ref, other_ref)[side]
        row = (core if side == 0 else 1 - core) * half
        to = blocks.at[i, :, pl.ds(pl.multiple_of(row, half), half), :]
        return pltpu.make_async_copy(ref.at[i], to, arrived.at[side, i])

    for i in range(leaves):
        for side in range(2):
            fetch(i, side).start()
    for part, ref in enumerate((before_ref, packed_ref, after_ref)):
        for n in range(leaves):
            window[part * leaves + n] = ref[:, n * rows : (n + 1) * rows]
            at = leaves * rows + n * 2 * rank
            coefs[part * leaves + n] = ref[:, at : at + 2 * rank]
    window[3 * leaves] = jnp.zeros((cols, rows), BF16)
    coefs[3 * leaves] = jnp.zeros((cols, 2 * rank), BF16)
    for copy in lists:
        copy.wait()

    def slot(index):
        return jnp.where(index >= 0, jnp.clip(index - start, 0, 3 * leaves - 1), 3 * leaves)

    def far_leaf(i, carry):
        total = jnp.zeros((cols, 2 * rank), F32)
        for k in range(slots):
            total += dot_nt(coefs[slot(far_index_ref[i, k])], table_ref[far_kind_ref[i, k]])
        far_out_ref[i] = fold(total, rank)
        return carry

    def near_leaf(i, carry):
        for side in range(2):
            fetch(i, side).wait()
        total = jnp.zeros((cols, rows), F32)
        for k in range(slots):
            total += dot_nt(window[slot(near_ref[i, k])], blocks[i, k])
        near_out_ref[:, pl.ds(pl.multiple_of(i * rows, rows), rows)] = total
        return carry

    lax.fori_loop(0, leaves, far_leaf, 0)
    lax.fori_loop(0, leaves, near_leaf, 0)


def last_kernel(seen_ref, high_ref, own_ref, spread_ref, far_ref, near_ref, basis_ref, out_ref):
    count = seen_ref.shape[0]
    leaves, rank, rows = basis_ref.shape
    total = dot(unlanes(seen_ref[0]), high_ref[0])
    for j in range(1, count):
        total += dot(unlanes(seen_ref[j]), high_ref[j])
    group = triple_left(own_ref[...] + fold(total, rank))
    for i in range(leaves):
        field = (dot(group, spread_ref[i]) + far_ref[i]).astype(BF16)
        at = slice(i * rows, (i + 1) * rows)
        out_ref[:, at] = (near_ref[:, at] + dot(field, basis_ref[i])).astype(BF16)


def call(kernel, outs, ins, flops, moved, mib, scratch=()):
    def spec(space):
        return pl.BlockSpec(memory_space=space)

    many = isinstance(outs, tuple)
    return pl.pallas_call(
        kernel,
        out_shape=outs,
        in_specs=[spec(space) for space in ins],
        out_specs=tuple(spec(pltpu.VMEM) for _ in outs) if many else spec(pltpu.VMEM),
        scratch_shapes=list(scratch),
        compiler_params=pltpu.CompilerParams(vmem_limit_bytes=mib << 20),
        cost_estimate=pl.CostEstimate(flops=flops, bytes_accessed=moved, transcendentals=0),
    )


def shards(
    vectors, near_blocks, near_index, far_index, far_kind,
    cluster_basis, leaf_transfer, coupling_table, parent_transfer_matrices, coarse_kind,
):
    cols, width = vectors.shape
    leaves, rank, rows = cluster_basis.shape
    slots = near_index.shape[1]
    kinds = coupling_table.shape[0]
    peers = lax.axis_size("leaf")
    half = (peers.bit_length() - 1) // 2
    size = 1 << half
    shape = jax.ShapeDtypeStruct
    packed_width = width + leaves * 2 * rank
    vm, hbm = pltpu.VMEM, pltpu.HBM
    kept = lambda space, array: space(array.shape, array.dtype)
    sems = lambda *count: pltpu.SemaphoreType.DMA(count)
    message = shape((size, cols // 2, 2 * rank), BF16)
    low_groups = [[n * size + j for j in range(size)] for n in range(size)]
    high_groups = [[n * size + j for n in range(size)] for j in range(size)]
    up = [(n, n + 1) for n in range(peers - 1)]
    stay = lambda *arrays: [pltpu.with_memory_space_constraint(a, hbm) for a in arrays]
    (
        vectors, blocks_here, near_index, far_index, far_kind, basis_here, transfer_here,
        coupling_table, parent_transfer_matrices, coarse_kind,
    ) = stay(
        vectors, near_blocks, near_index, far_index, far_kind, cluster_basis, leaf_transfer,
        coupling_table, parent_transfer_matrices, coarse_kind,
    )

    packed, group = call(
        coef_kernel, (shape((cols, packed_width), BF16), message),
        [hbm] * 3, 2**26, 2**20, 4,
        [kept(vm, vectors), kept(vm, cluster_basis), kept(vm, leaf_transfer), sems(3)],
    )(vectors, basis_here, transfer_here)
    seen_low = lax.all_to_all(
        group, "leaf", 0, 0, axis_index_groups=low_groups, tiled=True
    )
    before = lax.ppermute(packed, "leaf", up)
    after = lax.ppermute(packed, "leaf", [(b, a) for a, b in up])
    other_blocks = lax.ppermute(near_blocks, "cols", [(0, 1), (1, 0)])
    low_table, down = call(
        low_path_kernel,
        (shape((size, rank, 4 * rank), BF16), shape((rank, rank), F32)),
        [hbm] * 3, 2**27, 2**20, 6,
        [
            kept(pltpu.SMEM, coarse_kind), kept(vm, coupling_table),
            kept(vm, parent_transfer_matrices), sems(3),
        ],
    )(coarse_kind, coupling_table, parent_transfer_matrices)
    own, sent = call(
        middle_kernel, (shape((cols, rank), F32), message),
        [vm] * 2, 2**25, 2**19, 4,
    )(seen_low, low_table)
    seen_high = lax.all_to_all(sent, "leaf", 0, 0, axis_index_groups=high_groups, tiled=True)
    high_table, far_table, spread = call(
        high_path_kernel,
        (
            shape((size, rank, 2 * rank), BF16),
            shape((kinds, 2 * rank, 2 * rank), BF16),
            shape((leaves, 3 * rank, rank), BF16),
        ),
        [hbm] * 4 + [vm], 2**27, 2**20, 8,
        [
            kept(pltpu.SMEM, coarse_kind), kept(vm, coupling_table),
            kept(vm, parent_transfer_matrices), kept(vm, leaf_transfer), sems(4),
        ],
    )(coarse_kind, coupling_table, parent_transfer_matrices, transfer_here, down)
    near, far = call(
        near_kernel,
        (shape((cols, width), F32), shape((leaves, cols, rank), F32)),
        [hbm] * 3 + [vm] * 3 + [hbm] * 2 + [vm], 2**30, 10 * 2**20, 16,
        [
            pltpu.VMEM((3 * leaves + 1, cols, rows), BF16),
            pltpu.VMEM((3 * leaves + 1, cols, 2 * rank), BF16),
            pltpu.VMEM((leaves, slots, rows, rows), BF16),
            sems(2, leaves),
            kept(pltpu.SMEM, near_index), kept(pltpu.SMEM, far_index),
            kept(pltpu.SMEM, far_kind), sems(3),
        ],
    )(
        near_index, far_index, far_kind,
        before, packed, after, blocks_here, stay(other_blocks)[0], far_table,
    )
    return call(
        last_kernel, shape((cols, width), BF16), [vm] * 7, 2**27, 2**21, 8
    )(seen_high, high_table, own, spread, far, near, cluster_basis)


def solution(mesh):
    in_specs = (
        P("cols", "leaf"),
        P("leaf", None, "cols", None),
        P("leaf", None),
        P("leaf", None),
        P("leaf", None),
        P("leaf", None, None),
        P("leaf", None, None),
        P(),
        P(),
        P(),
    )
    out_specs = P("cols", "leaf")
    return jax.shard_map(shards, mesh=mesh, in_specs=in_specs, out_specs=out_specs, check_vma=False)
```

profile of v0, /device:TPU:24, one launch (start us, length us, event | category | flops | bytes accessed | tf_op | source)
XLA Modules:
  0.0 59.8 jit_solution(5633709689095656880)
XLA Ops:
  0.0 1.9 %collective-permute-start.2 = (bf16[8,8,128,256]{3,2,1,0:T(8,128)(2,1)}, bf16[8,8,128,256]{3,2,1,0:T(8,128)(2,1)}, u32[]{:S(2)}, u32[]{:S(2)}) collective-permute-start(bf16[8,8,128,256]{3,2,1,0:T(8,128)(2,1)} %own_ref.1), channel_id=1, source_target_pairs={{0,1},{1,0},{2,3},{3,2},{4,5},{5,4},{6,7},{7,6},{8,9},{9,8},{10,11... | collective-permute-start | bytes 12582920 | tf_op jit(solution)/shard_map/ppermute | solution.py:316
  1.9 2.7 %shard_map.100 = (bf16[64,3072]{1,0:T(8,128)(2,1)S(1)}, bf16[16,32,128]{2,1,0:T(8,128)(2,1)}) custom-call(bf16[64,2048]{1,0:T(8,128)(2,1)} %x_hbm.1, bf16[8,64,256]{2,1,0:T(8,128)(2,1)} %basis_ref.1, f32[8,64,64]{2,1,0:T(8,128)} %transfer_hbm.3), custom_call_target="tpu_custom_call" | custom-call | flops 67108864 | bytes 1048576 | tf_op jit(solution)/shard_map/pallas_call | solution.py:306
  4.6 8.9 %all-to-all-start = ((bf16[16,32,128]{2,1,0:T(8,128)(2,1)}), bf16[16,32,128]{2,1,0:T(8,128)(2,1)S(1)}, u32[]{:S(2)}, u32[]{:S(2)}) async-start(bf16[16,32,128]{2,1,0:T(8,128)(2,1)} %get-tuple-element.16), calls=%async_computation | async-start | bytes 262144 | tf_op jit(solution)/shard_map/all_to_all | solution.py:311
  13.5 2.7 %collective-permute-start.1 = (bf16[64,3072]{1,0:T(8,128)(2,1)S(1)}, bf16[64,3072]{1,0:T(8,128)(2,1)S(1)}, u32[]{:S(2)}, u32[]{:S(2)}) collective-permute-start(bf16[64,3072]{1,0:T(8,128)(2,1)S(1)} %get-tuple-element.23.packed_ref), channel_id=1, source_target_pairs={{2,0},{4,2},{6,4},{8,6},{10,8},{12,10},{14,12},{16,14},{18,16},{20... | collective-permute-start | bytes 1179656 | tf_op jit(solution)/shard_map/ppermute | solution.py:315
  16.3 5.2 %collective-permute-start = (bf16[64,3072]{1,0:T(8,128)(2,1)S(1)}, bf16[64,3072]{1,0:T(8,128)(2,1)S(1)}, u32[]{:S(2)}, u32[]{:S(2)}) collective-permute-start(bf16[64,3072]{1,0:T(8,128)(2,1)S(1)} %get-tuple-element.23.packed_ref), channel_id=1, source_target_pairs={{0,2},{2,4},{4,6},{6,8},{8,10},{10,12},{12,14},{14,16},{16,18},{18... | collective-permute-start | bytes 1179656 | tf_op jit(solution)/shard_map/ppermute | solution.py:314
  21.5 2.5 %shard_map.101 = (bf16[16,64,256]{2,1,0:T(8,128)(2,1)S(1)}, f32[64,64]{1,0:T(8,128)S(1)}) custom-call(s32[255]{0:T(256)} %kind_hbm.3, f32[16,64,64]{2,1,0:T(8,128)} %table_hbm.3, f32[2,64,64]{2,1,0:T(8,128)} %parent_hbm.3), custom_call_target="tpu_custom_call" | custom-call | flops 134217728 | bytes 1048576 | tf_op jit(solution)/shard_map/pallas_call | solution.py:317
  24.0 0.0 all-to-all-done.seen_ref
  24.0 1.1 %shard_map.102 = (f32[64,64]{1,0:T(8,128)S(1)}, bf16[16,32,128]{2,1,0:T(8,128)(2,1)}) custom-call(bf16[16,32,128]{2,1,0:T(8,128)(2,1)S(1)} %all-to-all-done.seen_ref, bf16[16,64,256]{2,1,0:T(8,128)(2,1)S(1)} %get-tuple-element.17.low_ref), custom_call_target="tpu_custom_call" | custom-call | flops 33554432 | bytes 524288 | tf_op jit(solution)/shard_map/pallas_call | solution.py:326
  25.2 14.8 %all-to-all-start.1 = ((bf16[16,32,128]{2,1,0:T(8,128)(2,1)}), bf16[16,32,128]{2,1,0:T(8,128)(2,1)S(1)}, u32[]{:S(2)}, u32[]{:S(2)}) async-start(bf16[16,32,128]{2,1,0:T(8,128)(2,1)} %get-tuple-element.18), calls=%async_computation.1 | async-start | bytes 262144 | tf_op jit(solution)/shard_map/all_to_all | solution.py:330
  40.0 2.7 %shard_map.103 = (bf16[16,64,128]{2,1,0:T(8,128)(2,1)S(1)}, bf16[16,128,128]{2,1,0:T(8,128)(2,1)S(1)}, bf16[8,192,64]{2,1,0:T(8,128)(2,1)S(1)}) custom-call(s32[255]{0:T(256)} %kind_hbm.3, f32[16,64,64]{2,1,0:T(8,128)} %table_hbm.3, f32[2,64,64]{2,1,0:T(8,128)} %parent_hbm.3, f32[8,64,64]{2,1,0:T(8,128)} %transfer_hbm.3, f32[64,64]{1,0:T(8,128)S(1)} %get-tuple-element.19.down_ref), custom_call_target="tpu_custom_call" | custom-call | flops 134217728 | bytes 1048576 | tf_op jit(solution)/shard_map/pallas_call | solution.py:331
  42.7 0.0 collective-permute-done.1.after_ref
  42.7 0.0 collective-permute-done.before_ref
  42.7 0.0 collective-permute-done.2.other_ref
  42.7 0.0 copy-start
  42.8 7.5 %shard_map.104 = (f32[64,2048]{1,0:T(8,128)S(1)}, f32[8,64,64]{2,1,0:T(8,128)S(1)}) custom-call(s32[8,8]{1,0:T(8,128)} %near_hbm.1, s32[8,8]{1,0:T(8,128)} %far_index_hbm.1, s32[8,8]{1,0:T(8,128)} %far_kind_hbm.1, bf16[64,3072]{1,0:T(8,128)(2,1)S(1)} %collective-permute-done.before_ref, bf16[64,3072]{1,0:T(8,128)(2,1)S(1)} %get-tuple-element.23.packed_ref, ...), custom_call_target="tpu_custom_call" | custom-call | flops 1073741824 | bytes 10485760 | tf_op jit(solution)/shard_map/pallas_call | solution.py:344
  50.3 7.2 %all-to-all-done.1.seen_ref = bf16[16,32,128]{2,1,0:T(8,128)(2,1)S(1)} async-done(((bf16[16,32,128]{2,1,0:T(8,128)(2,1)}), bf16[16,32,128]{2,1,0:T(8,128)(2,1)S(1)}, u32[]{:S(2)}, u32[]{:S(2)}) %all-to-all-start.1) | async-done | bytes 131104 | tf_op jit(solution)/shard_map/all_to_all | solution.py:330
  57.5 0.0 copy-done
  57.5 2.3 %shard_map.105 = bf16[64,2048]{1,0:T(8,128)(2,1)} custom-call(bf16[16,32,128]{2,1,0:T(8,128)(2,1)S(1)} %all-to-all-done.1.seen_ref, bf16[16,64,128]{2,1,0:T(8,128)(2,1)S(1)} %get-tuple-element.20.high_ref, f32[64,64]{1,0:T(8,128)S(1)} %get-tuple-element.21.own_ref, bf16[8,192,64]{2,1,0:T(8,128)(2,1)S(1)} %get-tuple-element.22.spread_ref, ...), custom_call_target="tpu_custom_call" | custom-call | flops 134217728 | bytes 2097152 | tf_op jit(solution)/shard_map/pallas_call | solution.py:360
Async XLA Ops:
  0.0 42.7 %collective-permute-start.2 = (bf16[8,8,128,256]{3,2,1,0:T(8,128)(2,1)}, bf16[8,8,128,256]{3,2,1,0:T(8,128)(2,1)}, u32[]{:S(2)}, u32[]{:S(2)}) collective-permute-start(bf16[8,8,128,256]{3,2,1,0:T(8,128)(2,1)} %own_ref.1), channel_id=1, source_target_pairs={{0,1},{1,0},{2,3},{3,2},{4,5},{5,4},{6,7},{7,6},{8,9},{9,8},{10,11... | collective-permute-start | bytes 12582920 | tf_op jit(solution)/shard_map/ppermute | solution.py:316
  4.6 19.4 %all-to-all-start = ((bf16[16,32,128]{2,1,0:T(8,128)(2,1)}), bf16[16,32,128]{2,1,0:T(8,128)(2,1)S(1)}, u32[]{:S(2)}, u32[]{:S(2)}) async-start(bf16[16,32,128]{2,1,0:T(8,128)(2,1)} %get-tuple-element.16), calls=%async_computation | async-start | bytes 262144 | tf_op jit(solution)/shard_map/all_to_all | solution.py:311
  13.5 29.2 %collective-permute-start.1 = (bf16[64,3072]{1,0:T(8,128)(2,1)S(1)}, bf16[64,3072]{1,0:T(8,128)(2,1)S(1)}, u32[]{:S(2)}, u32[]{:S(2)}) collective-permute-start(bf16[64,3072]{1,0:T(8,128)(2,1)S(1)} %get-tuple-element.23.packed_ref), channel_id=1, source_target_pairs={{2,0},{4,2},{6,4},{8,6},{10,8},{12,10},{14,12},{16,14},{18,16},{20... | collective-permute-start | bytes 1179656 | tf_op jit(solution)/shard_map/ppermute | solution.py:315
  16.3 26.4 %collective-permute-start = (bf16[64,3072]{1,0:T(8,128)(2,1)S(1)}, bf16[64,3072]{1,0:T(8,128)(2,1)S(1)}, u32[]{:S(2)}, u32[]{:S(2)}) collective-permute-start(bf16[64,3072]{1,0:T(8,128)(2,1)S(1)} %get-tuple-element.23.packed_ref), channel_id=1, source_target_pairs={{0,2},{2,4},{4,6},{6,8},{8,10},{10,12},{12,14},{14,16},{16,18},{18... | collective-permute-start | bytes 1179656 | tf_op jit(solution)/shard_map/ppermute | solution.py:314
  25.2 32.3 %all-to-all-start.1 = ((bf16[16,32,128]{2,1,0:T(8,128)(2,1)}), bf16[16,32,128]{2,1,0:T(8,128)(2,1)S(1)}, u32[]{:S(2)}, u32[]{:S(2)}) async-start(bf16[16,32,128]{2,1,0:T(8,128)(2,1)} %get-tuple-element.18), calls=%async_computation.1 | async-start | bytes 262144 | tf_op jit(solution)/shard_map/all_to_all | solution.py:330
  42.7 14.7 %copy-start = (bf16[8,64,256]{2,1,0:T(8,128)(2,1)S(1)}, bf16[8,64,256]{2,1,0:T(8,128)(2,1)}, u32[]{:S(2)}) copy-start(bf16[8,64,256]{2,1,0:T(8,128)(2,1)} %basis_ref.1) | copy-start | bytes 786436
where the time goes:
time: 60.2 us; the launch traced here: 59.8 us
  starting transfers between devices  33.6 us (56%)
  Pallas kernels  18.9 us (31%)
  waiting for transfers between devices  7.19 us (12%)
    all_to_all x1, starting transfers between devices, shards(): lax.all_to_all(sent, 'leaf', 0, 0, axis_index_groups=high_groups, tiled=T...  14.8 us
    all_to_all x1, starting transfers between devices, shards(): lax.all_to_all(group, 'leaf', 0, 0, axis_index_groups=low_groups, tiled=T...  8.89 us
    pallas_call x1, Pallas kernels, shards(): call(near_kernel, (shape((cols, width), F32), shape((leaves, cols, rank),...  7.54 us
    all_to_all x1, waiting for transfers between devices, shards(): lax.all_to_all(sent, 'leaf', 0, 0, axis_index_groups=high_groups, tiled=T...  7.18 us
    ppermute x1, starting transfers between devices, shards(): before = lax.ppermute(packed, 'leaf', up)  5.19 us
    ppermute x1, starting transfers between devices, shards(): after = lax.ppermute(packed, 'leaf', [(b, a) for a, b in up])  2.75 us
    pallas_call x1, Pallas kernels, shards(): call(coef_kernel, (shape((cols, packed_width), BF16), message), [hbm] * 3...  2.72 us
    pallas_call x1, Pallas kernels, shards(): call(high_path_kernel, (shape((size, rank, 2 * rank), BF16), shape((kinds...  2.68 us
  transfers between devices with their start and end apart: 5, of which 1 were waited for; matrix products, arithmetic and copies ran while one was open for 0% of the time, Pallas kernels for 28%

commit v1 on v0

v1 whole, which is shorter than its diff:
```python
import jax
import jax.numpy as jnp
from jax import lax
from jax.experimental import pallas as pl
from jax.experimental.pallas import tpu as pltpu
from jax.sharding import PartitionSpec as P


F32 = jnp.float32
BF16 = jnp.bfloat16
Y_BITS, Z_BITS, X_BITS = 2, 4, 2
NT = (((1,), (1,)), ((), ()))


def halves(value):
    high = value.astype(BF16)
    return high, (value - high.astype(F32)).astype(BF16)


def triple_left(value):
    high, low = halves(value)
    return jnp.concatenate([high, low, high], axis=1)


def triple_right(value):
    high, low = halves(value)
    return jnp.concatenate([high, high, low], axis=0)


def dot(left, right):
    return jnp.dot(left, right, preferred_element_type=F32)


def dot_nt(left, right):
    return lax.dot_general(left, right, NT, preferred_element_type=F32)


def fold(value, rank):
    return value[:, :rank] + value[:, rank : 2 * rank]


def lanes(value):
    part = value.shape[0] // 2
    return jnp.concatenate([value[:part], value[part:]], axis=1)


def unlanes(value):
    rank = value.shape[1] // 2
    return jnp.concatenate([value[:, :rank], value[:, rank:]], axis=0)


def bring(sources, targets, arrived):
    copies = [
        pltpu.make_async_copy(source, target, arrived.at[n])
        for n, (source, target) in enumerate(zip(sources, targets))
    ]
    for copy in copies:
        copy.start()
    return copies


def coef_kernel(
    x_hbm, basis_hbm, transfer_hbm, parent_hbm, packed_ref, group_ref, own_ref,
    x_ref, basis_ref, transfer_ref, parent_ref, arrived,
):
    leaves, rank, rows = basis_ref.shape
    copies = bring(
        (parent_hbm, x_hbm, basis_hbm, transfer_hbm),
        (parent_ref, x_ref, basis_ref, transfer_ref),
        arrived,
    )
    g = lax.axis_index("leaf")
    copies[0].wait()
    rise = None
    for level in range(Y_BITS):
        step = jnp.where(((g >> level) & 1) == 1, parent_ref[1], parent_ref[0])
        rise = step if rise is None else dot(triple_left(step), triple_right(rise))
    rise = triple_right(rise.T)
    for copy in copies[1:3]:
        copy.wait()
    packed_ref[:, : leaves * rows] = x_ref[...]
    pairs = []
    for i in range(leaves):
        high, low = halves(dot_nt(x_ref[:, i * rows : (i + 1) * rows], basis_ref[i]))
        both = jnp.concatenate([high, low], axis=1)
        start = leaves * rows + i * 2 * rank
        packed_ref[:, start : start + 2 * rank] = both
        pairs.append((high, both))
    copies[3].wait()
    total = jnp.zeros((x_ref.shape[0], rank), F32)
    for i, (high, both) in enumerate(pairs):
        above, below = halves(transfer_ref[i])
        total += dot_nt(both, jnp.concatenate([above, above], axis=1)) + dot_nt(high, below)
    sent = lanes(dot(triple_left(total), rise).astype(BF16))
    for j in range(group_ref.shape[0]):
        group_ref[j] = sent
    own_ref[...] = lanes(total.astype(BF16))


def path_blocks(g, groups, first, last, down, kind_ref, table_ref, parent_ref, with_sum):
    rank = table_ref.shape[1]
    steps = [triple_left(parent_ref[0]), triple_left(parent_ref[1])]
    across = []
    for level in range(first, last):
        heap = (groups >> (level + 1)) + (g >> (level + 1))
        coupling = table_ref[kind_ref[heap - 1]]
        bit = (g >> level) & 1
        coupling = jnp.where(bit == 1, coupling, coupling.T)
        step = jnp.where(bit == 1, parent_ref[1], parent_ref[0])
        if down is None:
            across.append(coupling)
            down = step
        else:
            right = triple_right(down)
            made = dot(triple_left(jnp.concatenate([coupling, step], axis=0)), right)
            across.append(made[:rank])
            down = made[rank:]
    upward = jnp.concatenate([parent_ref[0].T, parent_ref[1].T], axis=0)
    left = triple_left(upward)
    trees = [[block] for block in across]
    if with_sum:
        trees.append([upward[:rank], upward[rank:]])
    for step in range(1, last - first):
        live = [t for t in range(len(trees)) if t >= step]
        blocks = [block for t in live for block in trees[t]]
        made = dot(left, triple_right(jnp.concatenate(blocks, axis=1)))
        at = 0
        for t in live:
            grown = []
            for _ in trees[t]:
                for b in range(2):
                    grown.append(made[b * rank : (b + 1) * rank, at * rank : (at + 1) * rank])
                at += 1
            trees[t] = grown
    return trees, down


def store_blocks(trees, here, ref, offset):
    rank = ref.shape[1]
    ref[offset + here, :, : 2 * rank] = jnp.zeros((rank, 2 * rank), BF16)
    for t, blocks in enumerate(trees):
        base = ((here >> t) ^ 1) << t
        for v, block in enumerate(blocks):
            ref[offset + base + v, :, : 2 * rank] = jnp.concatenate(halves(block), axis=1)


def path_kernel(
    kind_hbm, table_hbm, parent_hbm, transfer_hbm, z_ref, yx_ref, fall_ref, far_ref, spread_ref,
    kind_ref, table_ref, parent_ref, transfer_ref, arrived,
):
    for copy in bring(
        (kind_hbm, table_hbm, parent_hbm, transfer_hbm),
        (kind_ref, table_ref, parent_ref, transfer_ref),
        arrived,
    ):
        copy.wait()
    g = lax.axis_index("leaf")
    groups = kind_ref.shape[0] + 1
    rank = table_ref.shape[1]
    low, high = Y_BITS, Y_BITS + Z_BITS
    tree = (kind_ref, table_ref, parent_ref)

    trees, inner = path_blocks(g, groups, low, high, None, *tree, True)
    store_blocks(trees[:Z_BITS], (g >> low) & ((1 << Z_BITS) - 1), z_ref, 0)
    for j, block in enumerate(trees[Z_BITS]):
        z_ref[j, :, 2 * rank :] = jnp.concatenate(halves(block), axis=1)

    y_trees, fall = path_blocks(g, groups, 0, low, None, *tree, False)
    fall_ref[...] = jnp.concatenate(halves(fall), axis=1)
    down = dot(triple_left(inner), triple_right(fall))
    x_trees, _ = path_blocks(g, groups, high, high + X_BITS, down, *tree, False)
    here = g >> high
    for t, blocks in enumerate(x_trees):
        base = ((here >> t) ^ 1) << t
        for v, block in enumerate(blocks):
            both = jnp.concatenate(halves(block), axis=1)
            for y in range(1 << Y_BITS):
                yx_ref[((base + v) << Y_BITS) + y] = both
    store_blocks(y_trees, g & ((1 << Y_BITS) - 1), yx_ref, here << Y_BITS)

    for kind in range(table_ref.shape[0]):
        above, below = halves(table_ref[kind])
        far_ref[kind, :rank, :] = jnp.concatenate([above, above], axis=1)
        far_ref[kind, rank:, :] = jnp.concatenate([below, jnp.zeros_like(below)], axis=1)
    for i in range(transfer_ref.shape[0]):
        spread_ref[i] = triple_right(transfer_ref[i])


def middle_kernel(seen_ref, z_ref, own_ref, sent_ref):
    count = seen_ref.shape[0]
    rank = z_ref.shape[1]
    rows = own_ref.shape[0]
    total = dot(unlanes(seen_ref[0]), z_ref[0])
    for j in range(1, count):
        total += dot(unlanes(seen_ref[j]), z_ref[j])
    inside = lanes(fold(total[:, : 2 * rank], rank).astype(BF16))
    outside = lanes(fold(total[:, 2 * rank :], rank).astype(BF16))
    own = own_ref[...]
    here = lax.axis_index("leaf") >> (Y_BITS + Z_BITS)
    for x in range(1 << X_BITS):
        mine = here == x
        first, second = jnp.where(mine, own, outside), jnp.where(mine, inside, outside)
        for y in range(1 << Y_BITS):
            sent_ref[(x << Y_BITS) + y, :rows] = first
            sent_ref[(x << Y_BITS) + y, rows:] = second


def near_kernel(
    near_hbm, far_index_hbm, far_kind_hbm,
    before_ref, packed_ref, after_ref, own_ref, other_ref, table_ref,
    out_ref, window, coefs, blocks, arrived,
    near_ref, far_index_ref, far_kind_ref, lists_arrived,
):
    lists = bring(
        (near_hbm, far_index_hbm, far_kind_hbm), (near_ref, far_index_ref, far_kind_ref),
        lists_arrived,
    )
    leaves, slots, half, rows = own_ref.shape
    cols = packed_ref.shape[0]
    rank = coefs.shape[2] // 2
    start = (lax.axis_index("leaf") - 1) * leaves
    core = lax.axis_index("cols")

    def fetch(i, side):
        ref = (own_ref, other_ref)[side]
        row = (core if side == 0 else 1 - core) * half
        to = blocks.at[i, :, pl.ds(pl.multiple_of(row, half), half), :]
        return pltpu.make_async_copy(ref.at[i], to, arrived.at[side, i])

    for i in range(leaves):
        for side in range(2):
            fetch(i, side).start()
    for part, ref in enumerate((before_ref, packed_ref, after_ref)):
        for n in range(leaves):
            window[part * leaves + n] = ref[:, n * rows : (n + 1) * rows]
            at = leaves * rows + n * 2 * rank
            coefs[part * leaves + n] = ref[:, at : at + 2 * rank]
    window[3 * leaves] = jnp.zeros((cols, rows), BF16)
    coefs[3 * leaves] = jnp.zeros((cols, 2 * rank), BF16)
    for copy in lists:
        copy.wait()

    def slot(index):
        return jnp.where(index >= 0, jnp.clip(index - start, 0, 3 * leaves - 1), 3 * leaves)

    def far_leaf(i):
        total = jnp.zeros((cols, 2 * rank), F32)
        for k in range(slots):
            total += dot_nt(coefs[slot(far_index_ref[i, k])], table_ref[far_kind_ref[i, k]])
        return fold(total, rank)

    for i in range(0, leaves, 2):
        at = leaves * rows + i * rank
        out_ref[:, at : at + 2 * rank] = jnp.concatenate([far_leaf(i), far_leaf(i + 1)], axis=1)
    for i in range(leaves):
        if i % 2 == 0:
            for n in (i, i + 1):
                for side in range(2):
                    fetch(n, side).wait()
        total = jnp.zeros((cols, rows), F32)
        for k in range(slots):
            total += dot_nt(window[slot(near_ref[i, k])], blocks[i, k])
        out_ref[:, i * rows : (i + 1) * rows] = total


def last_kernel(seen_ref, yx_ref, fall_ref, spread_ref, local_ref, basis_ref, out_ref):
    count, rows, _ = seen_ref.shape
    leaves, rank, width = basis_ref.shape
    half = rows // 2
    start = (lax.axis_index("leaf") >> (Y_BITS + Z_BITS)) << Y_BITS
    total = dot(unlanes(seen_ref[0, :half]), yx_ref[0])
    for j in range(1, count):
        total += dot(unlanes(seen_ref[j, :half]), yx_ref[j])
    for y in range(1 << Y_BITS):
        total += dot(unlanes(seen_ref[start + y, half:]), fall_ref[...])
    group = triple_left(fold(total, rank))
    for i in range(leaves):
        far = local_ref[:, leaves * width + i * rank : leaves * width + (i + 1) * rank]
        field = (dot(group, spread_ref[i]) + far).astype(BF16)
        at = slice(i * width, (i + 1) * width)
        out_ref[:, at] = (local_ref[:, at] + dot(field, basis_ref[i])).astype(BF16)


def call(kernel, outs, ins, flops, moved, mib, scratch=()):
    def spec(space):
        return pl.BlockSpec(memory_space=space)

    many = isinstance(outs, tuple)
    return pl.pallas_call(
        kernel,
        out_shape=outs,
        in_specs=[spec(space) for space in ins],
        out_specs=tuple(spec(pltpu.VMEM) for _ in outs) if many else spec(pltpu.VMEM),
        scratch_shapes=list(scratch),
        compiler_params=pltpu.CompilerParams(vmem_limit_bytes=mib << 20),
        cost_estimate=pl.CostEstimate(flops=flops, bytes_accessed=moved, transcendentals=0),
    )


def shards(
    vectors, near_blocks, near_index, far_index, far_kind,
    cluster_basis, leaf_transfer, coupling_table, parent_transfer_matrices, coarse_kind,
):
    cols, width = vectors.shape
    leaves, rank, rows = cluster_basis.shape
    slots = near_index.shape[1]
    kinds = coupling_table.shape[0]
    peers = lax.axis_size("leaf")
    size = 1 << Z_BITS
    across = 1 << (X_BITS + Y_BITS)
    shape = jax.ShapeDtypeStruct
    packed_width = width + leaves * 2 * rank
    vm, hbm = pltpu.VMEM, pltpu.HBM
    kept = lambda space, array: space(array.shape, array.dtype)
    sems = lambda *count: pltpu.SemaphoreType.DMA(count)
    own_line = shape((cols // 2, 2 * rank), BF16)
    line = (1 << Z_BITS) - 1
    z_groups, yx_groups = {}, {}
    for n in range(peers):
        z_groups.setdefault(n & ~(line << Y_BITS), []).append(n)
        yx_groups.setdefault((n >> Y_BITS) & line, []).append(n)
    z_groups, yx_groups = list(z_groups.values()), list(yx_groups.values())
    up = [(n, n + 1) for n in range(peers - 1)]
    stay = lambda *arrays: [pltpu.with_memory_space_constraint(a, hbm) for a in arrays]
    (
        vectors, blocks_here, near_index, far_index, far_kind, basis_here, transfer_here,
        coupling_table, parent_transfer_matrices, coarse_kind,
    ) = stay(
        vectors, near_blocks, near_index, far_index, far_kind, cluster_basis, leaf_transfer,
        coupling_table, parent_transfer_matrices, coarse_kind,
    )

    packed, group, own = call(
        coef_kernel,
        (
            shape((cols, packed_width), BF16),
            shape((size, *own_line.shape), BF16),
            own_line,
        ),
        [hbm] * 4, 2**26, 2**20, 4,
        [
            kept(vm, vectors), kept(vm, cluster_basis), kept(vm, leaf_transfer),
            kept(vm, parent_transfer_matrices), sems(4),
        ],
    )(vectors, basis_here, transfer_here, parent_transfer_matrices)
    seen_z = lax.all_to_all(group, "leaf", 0, 0, axis_index_groups=z_groups, tiled=True)
    before = lax.ppermute(packed, "leaf", up)
    after = lax.ppermute(packed, "leaf", [(b, a) for a, b in up])
    other_blocks = lax.ppermute(near_blocks, "cols", [(0, 1), (1, 0)])
    z_table, yx_table, fall, far_table, spread = call(
        path_kernel,
        (
            shape((size, rank, 4 * rank), BF16),
            shape((across, rank, 2 * rank), BF16),
            shape((rank, 2 * rank), BF16),
            shape((kinds, 2 * rank, 2 * rank), BF16),
            shape((leaves, 3 * rank, rank), BF16),
        ),
        [hbm] * 4, 2**28, 2**20, 8,
        [
            kept(pltpu.SMEM, coarse_kind), kept(vm, coupling_table),
            kept(vm, parent_transfer_matrices), kept(vm, leaf_transfer), sems(4),
        ],
    )(coarse_kind, coupling_table, parent_transfer_matrices, transfer_here)
    sent = call(
        middle_kernel, shape((across, cols, 2 * rank), BF16),
        [vm] * 3, 2**25, 2**19, 4,
    )(seen_z, z_table, own)
    seen_yx = lax.all_to_all(sent, "leaf", 0, 0, axis_index_groups=yx_groups, tiled=True)
    local = call(
        near_kernel,
        shape((cols, width + leaves * rank), F32),
        [hbm] * 3 + [vm] * 3 + [hbm] * 2 + [vm], 2**30, 10 * 2**20, 16,
        [
            pltpu.VMEM((3 * leaves + 1, cols, rows), BF16),
            pltpu.VMEM((3 * leaves + 1, cols, 2 * rank), BF16),
            pltpu.VMEM((leaves, slots, rows, rows), BF16),
            sems(2, leaves),
            kept(pltpu.SMEM, near_index), kept(pltpu.SMEM, far_index),
            kept(pltpu.SMEM, far_kind), sems(3),
        ],
    )(
        near_index, far_index, far_kind,
        before, packed, after, blocks_here, stay(other_blocks)[0], far_table,
    )
    return call(
        last_kernel, shape((cols, width), BF16), [vm] * 6, 2**27, 2**21, 8
    )(seen_yx, yx_table, fall, spread, local, cluster_basis)


def solution(mesh):
    in_specs = (
        P("cols", "leaf"),
        P("leaf", None, "cols", None),
        P("leaf", None),
        P("leaf", None),
        P("leaf", None),
        P("leaf", None, None),
        P("leaf", None, None),
        P(),
        P(),
        P(),
    )
    out_specs = P("cols", "leaf")
    return jax.shard_map(shards, mesh=mesh, in_specs=in_specs, out_specs=out_specs, check_vma=False)
```

time: 60.2 us -> 53.9 us (0.90)
  the two profiles are of different devices: /device:TPU:24 before, /device:TPU:32 now
where the time goes in v1:
time: 53.9 us; the launch traced here: 53.5 us
  starting transfers between devices  30.5 us (57%)
  Pallas kernels  15.5 us (29%)
  waiting for transfers between devices  7.33 us (14%)
    all_to_all x1, starting transfers between devices, shards(): lax.all_to_all(group, 'leaf', 0, 0, axis_index_groups=z_groups, tiled=True)  15.2 us
    all_to_all x1, starting transfers between devices, shards(): lax.all_to_all(sent, 'leaf', 0, 0, axis_index_groups=yx_groups, tiled=True)  7.03 us
    pallas_call x1, Pallas kernels, shards(): call(near_kernel, shape((cols, width + leaves * rank), F32), [hbm] * 3 +...  5.84 us
    all_to_all x1, waiting for transfers between devices, shards(): lax.all_to_all(group, 'leaf', 0, 0, axis_index_groups=z_groups, tiled=True)  4.75 us
    ppermute x1, starting transfers between devices, shards(): after = lax.ppermute(packed, 'leaf', [(b, a) for a, b in up])  4.46 us
    pallas_call x1, Pallas kernels, shards(): call(path_kernel, (shape((size, rank, 4 * rank), BF16), shape((across, ra...  3.32 us
    pallas_call x1, Pallas kernels, shards(): call(coef_kernel, (shape((cols, packed_width), BF16), shape((size, *own_l...  2.85 us
    all_to_all x1, waiting for transfers between devices, shards(): lax.all_to_all(sent, 'leaf', 0, 0, axis_index_groups=yx_groups, tiled=True)  2.57 us
  transfers between devices with their start and end apart: 5, of which 2 were waited for; matrix products, arithmetic and copies ran while one was open for 0% of the time, Pallas kernels for 25%

profile of v1, /device:TPU:32, one launch (start us, length us, event | category | flops | bytes accessed | tf_op | source)
XLA Modules:
  0.0 53.5 jit_solution(15308661262016830958)
XLA Ops:
  0.0 1.9 %collective-permute-start.2 = (bf16[8,8,128,256]{3,2,1,0:T(8,128)(2,1)}, bf16[8,8,128,256]{3,2,1,0:T(8,128)(2,1)}, u32[]{:S(2)}, u32[]{:S(2)}) collective-permute-start(bf16[8,8,128,256]{3,2,1,0:T(8,128)(2,1)} %own_ref.1), channel_id=1, source_target_pairs={{0,1},{1,0},{2,3},{3,2},{4,5},{5,4},{6,7},{7,6},{8,9},{9,8},{10,11... | collective-permute-start | bytes 12582920 | tf_op jit(solution)/shard_map/ppermute | solution.py:349
  1.9 2.8 %shard_map.100 = (bf16[64,3072]{1,0:T(8,128)(2,1)S(1)}, bf16[16,32,128]{2,1,0:T(8,128)(2,1)}, bf16[32,128]{1,0:T(8,128)(2,1)S(1)}) custom-call(bf16[64,2048]{1,0:T(8,128)(2,1)} %x_hbm.1, bf16[8,64,256]{2,1,0:T(8,128)(2,1)} %basis_ref.1, f32[8,64,64]{2,1,0:T(8,128)} %transfer_hbm.3, f32[2,64,64]{2,1,0:T(8,128)} %parent_hbm.3), custom_call_target="tpu_custom_call" | custom-call | flops 67108864 | bytes 1048576 | tf_op jit(solution)/shard_map/pallas_call | solution.py:333
  4.8 15.2 %all-to-all-start = ((bf16[16,32,128]{2,1,0:T(8,128)(2,1)}), bf16[16,32,128]{2,1,0:T(8,128)(2,1)S(1)}, u32[]{:S(2)}, u32[]{:S(2)}) async-start(bf16[16,32,128]{2,1,0:T(8,128)(2,1)} %get-tuple-element.13), calls=%async_computation | async-start | bytes 262144 | tf_op jit(solution)/shard_map/all_to_all | solution.py:346
  20.0 4.5 %collective-permute-start.1 = (bf16[64,3072]{1,0:T(8,128)(2,1)S(1)}, bf16[64,3072]{1,0:T(8,128)(2,1)S(1)}, u32[]{:S(2)}, u32[]{:S(2)}) collective-permute-start(bf16[64,3072]{1,0:T(8,128)(2,1)S(1)} %get-tuple-element.19.packed_ref), channel_id=1, source_target_pairs={{2,0},{4,2},{6,4},{8,6},{10,8},{12,10},{14,12},{16,14},{18,16},{20... | collective-permute-start | bytes 1179656 | tf_op jit(solution)/shard_map/ppermute | solution.py:348
  24.5 1.9 %collective-permute-start = (bf16[64,3072]{1,0:T(8,128)(2,1)S(1)}, bf16[64,3072]{1,0:T(8,128)(2,1)S(1)}, u32[]{:S(2)}, u32[]{:S(2)}) collective-permute-start(bf16[64,3072]{1,0:T(8,128)(2,1)S(1)} %get-tuple-element.19.packed_ref), channel_id=1, source_target_pairs={{0,2},{2,4},{4,6},{6,8},{8,10},{10,12},{12,14},{14,16},{16,18},{18... | collective-permute-start | bytes 1179656 | tf_op jit(solution)/shard_map/ppermute | solution.py:347
  26.4 3.3 %shard_map.101 = (bf16[16,64,256]{2,1,0:T(8,128)(2,1)S(1)}, bf16[16,64,128]{2,1,0:T(8,128)(2,1)S(1)}, bf16[64,128]{1,0:T(8,128)(2,1)S(1)}, bf16[16,128,128]{2,1,0:T(8,128)(2,1)S(1)}, bf16[8,192,64]{2,1,0:T(8,128)(2,1)S(1)}) custom-call(s32[255]{0:T(256)} %kind_hbm.1, f32[16,64,64]{2,1,0:T(8,128)} %table_hbm.1, f32[2,64,64]{2,1,0:T(8,128)} %parent_hbm.3, ...), custom_call_target="tpu_custom_call" | custom-call | flops 268435456 | bytes 1048576 | tf_op jit(solution)/shard_map/pallas_call | solution.py:350
  29.7 4.7 %all-to-all-done.seen_ref = bf16[16,32,128]{2,1,0:T(8,128)(2,1)S(1)} async-done(((bf16[16,32,128]{2,1,0:T(8,128)(2,1)}), bf16[16,32,128]{2,1,0:T(8,128)(2,1)S(1)}, u32[]{:S(2)}, u32[]{:S(2)}) %all-to-all-start) | async-done | bytes 131104 | tf_op jit(solution)/shard_map/all_to_all | solution.py:346
  34.5 1.2 %shard_map.102 = bf16[16,64,128]{2,1,0:T(8,128)(2,1)} custom-call(bf16[16,32,128]{2,1,0:T(8,128)(2,1)S(1)} %all-to-all-done.seen_ref, bf16[16,64,256]{2,1,0:T(8,128)(2,1)S(1)} %get-tuple-element.14.z_ref, bf16[32,128]{1,0:T(8,128)(2,1)S(1)} %get-tuple-element.15.own_ref), custom_call_target="tpu_custom_call" | custom-call | flops 33554432 | bytes 524288 | tf_op jit(solution)/shard_map/pallas_call | solution.py:365
  35.7 7.0 %all-to-all-start.1 = ((bf16[16,64,128]{2,1,0:T(8,128)(2,1)}), bf16[16,64,128]{2,1,0:T(8,128)(2,1)S(1)}, u32[]{:S(2)}, u32[]{:S(2)}) async-start(bf16[16,64,128]{2,1,0:T(8,128)(2,1)} %shard_map.102), calls=%async_computation.1 | async-start | bytes 524288 | tf_op jit(solution)/shard_map/all_to_all | solution.py:369
  42.7 0.0 collective-permute-done.1.after_ref
  42.7 0.0 collective-permute-done.before_ref
  42.7 0.0 collective-permute-done.2.other_ref
  42.8 0.0 copy-start
  42.8 5.8 %shard_map.103.local_ref = f32[64,2560]{1,0:T(8,128)S(1)} custom-call(s32[8,8]{1,0:T(8,128)} %near_hbm.1, s32[8,8]{1,0:T(8,128)} %far_index_hbm.1, s32[8,8]{1,0:T(8,128)} %far_kind_hbm.1, bf16[64,3072]{1,0:T(8,128)(2,1)S(1)} %collective-permute-done.before_ref, bf16[64,3072]{1,0:T(8,128)(2,1)S(1)} %get-tuple-element.19.packed_ref, ...), custom_call_target="tpu_custom_call" | custom-call | flops 1073741824 | bytes 10485760 | tf_op jit(solution)/shard_map/pallas_call | solution.py:370
  48.6 2.6 %all-to-all-done.1.seen_ref = bf16[16,64,128]{2,1,0:T(8,128)(2,1)S(1)} async-done(((bf16[16,64,128]{2,1,0:T(8,128)(2,1)}), bf16[16,64,128]{2,1,0:T(8,128)(2,1)S(1)}, u32[]{:S(2)}, u32[]{:S(2)}) %all-to-all-start.1) | async-done | bytes 262176 | tf_op jit(solution)/shard_map/all_to_all | solution.py:369
  51.2 0.0 copy-done
  51.2 2.3 %shard_map.104 = bf16[64,2048]{1,0:T(8,128)(2,1)} custom-call(bf16[16,64,128]{2,1,0:T(8,128)(2,1)S(1)} %all-to-all-done.1.seen_ref, bf16[16,64,128]{2,1,0:T(8,128)(2,1)S(1)} %get-tuple-element.16.yx_ref, bf16[64,128]{1,0:T(8,128)(2,1)S(1)} %get-tuple-element.17.fall_ref, bf16[8,192,64]{2,1,0:T(8,128)(2,1)S(1)} %get-tuple-element.18.spread_ref, ...), custom_call_target="tpu_custom_call" | custom-call | flops 134217728 | bytes 2097152 | tf_op jit(solution)/shard_map/pallas_call | solution.py:386
Async XLA Ops:
  0.0 42.7 %collective-permute-start.2 = (bf16[8,8,128,256]{3,2,1,0:T(8,128)(2,1)}, bf16[8,8,128,256]{3,2,1,0:T(8,128)(2,1)}, u32[]{:S(2)}, u32[]{:S(2)}) collective-permute-start(bf16[8,8,128,256]{3,2,1,0:T(8,128)(2,1)} %own_ref.1), channel_id=1, source_target_pairs={{0,1},{1,0},{2,3},{3,2},{4,5},{5,4},{6,7},{7,6},{8,9},{9,8},{10,11... | collective-permute-start | bytes 12582920 | tf_op jit(solution)/shard_map/ppermute | solution.py:349
  4.8 29.7 %all-to-all-start = ((bf16[16,32,128]{2,1,0:T(8,128)(2,1)}), bf16[16,32,128]{2,1,0:T(8,128)(2,1)S(1)}, u32[]{:S(2)}, u32[]{:S(2)}) async-start(bf16[16,32,128]{2,1,0:T(8,128)(2,1)} %get-tuple-element.13), calls=%async_computation | async-start | bytes 262144 | tf_op jit(solution)/shard_map/all_to_all | solution.py:346
  20.0 22.7 %collective-permute-start.1 = (bf16[64,3072]{1,0:T(8,128)(2,1)S(1)}, bf16[64,3072]{1,0:T(8,128)(2,1)S(1)}, u32[]{:S(2)}, u32[]{:S(2)}) collective-permute-start(bf16[64,3072]{1,0:T(8,128)(2,1)S(1)} %get-tuple-element.19.packed_ref), channel_id=1, source_target_pairs={{2,0},{4,2},{6,4},{8,6},{10,8},{12,10},{14,12},{16,14},{18,16},{20... | collective-permute-start | bytes 1179656 | tf_op jit(solution)/shard_map/ppermute | solution.py:348
  24.5 18.3 %collective-permute-start = (bf16[64,3072]{1,0:T(8,128)(2,1)S(1)}, bf16[64,3072]{1,0:T(8,128)(2,1)S(1)}, u32[]{:S(2)}, u32[]{:S(2)}) collective-permute-start(bf16[64,3072]{1,0:T(8,128)(2,1)S(1)} %get-tuple-element.19.packed_ref), channel_id=1, source_target_pairs={{0,2},{2,4},{4,6},{6,8},{8,10},{10,12},{12,14},{14,16},{16,18},{18... | collective-permute-start | bytes 1179656 | tf_op jit(solution)/shard_map/ppermute | solution.py:347
  35.7 15.5 %all-to-all-start.1 = ((bf16[16,64,128]{2,1,0:T(8,128)(2,1)}), bf16[16,64,128]{2,1,0:T(8,128)(2,1)S(1)}, u32[]{:S(2)}, u32[]{:S(2)}) async-start(bf16[16,64,128]{2,1,0:T(8,128)(2,1)} %shard_map.102), calls=%async_computation.1 | async-start | bytes 524288 | tf_op jit(solution)/shard_map/all_to_all | solution.py:369
  42.8 8.4 %copy-start = (bf16[8,64,256]{2,1,0:T(8,128)(2,1)S(1)}, bf16[8,64,256]{2,1,0:T(8,128)(2,1)}, u32[]{:S(2)}) copy-start(bf16[8,64,256]{2,1,0:T(8,128)(2,1)} %basis_ref.1) | copy-start | bytes 786436

commit v2 on v1

--- a/solution.py
+++ b/solution.py
@@ -44,9 +44,11 @@
     return jnp.concatenate([value[:part], value[part:]], axis=1)
 
 
-def unlanes(value):
-    rank = value.shape[1] // 2
-    return jnp.concatenate([value[:, :rank], value[:, rank:]], axis=0)
+def unlanes(values):
+    rank = values[0].shape[1] // 2
+    above = jnp.concatenate([value[:, :rank] for value in values], axis=1)
+    below = jnp.concatenate([value[:, rank:] for value in values], axis=1)
+    return jnp.concatenate([above, below], axis=0)
 
 
 def bring(sources, targets, arrived):
@@ -76,21 +78,23 @@
         step = jnp.where(((g >> level) & 1) == 1, parent_ref[1], parent_ref[0])
         rise = step if rise is None else dot(triple_left(step), triple_right(rise))
     rise = triple_right(rise.T)
-    for copy in copies[1:3]:
+    for copy in copies[1:]:
         copy.wait()
+    spread, stacked = [], []
     packed_ref[:, : leaves * rows] = x_ref[...]
-    pairs = []
     for i in range(leaves):
         high, low = halves(dot_nt(x_ref[:, i * rows : (i + 1) * rows], basis_ref[i]))
         both = jnp.concatenate([high, low], axis=1)
         start = leaves * rows + i * 2 * rank
         packed_ref[:, start : start + 2 * rank] = both
-        pairs.append((high, both))
-    copies[3].wait()
-    total = jnp.zeros((x_ref.shape[0], rank), F32)
-    for i, (high, both) in enumerate(pairs):
+        spread.append(both)
+    for i in range(leaves):
         above, below = halves(transfer_ref[i])
-        total += dot_nt(both, jnp.concatenate([above, above], axis=1)) + dot_nt(high, below)
+        twice = jnp.concatenate([above, above], axis=1)
+        once = jnp.concatenate([below, jnp.zeros_like(below)], axis=1)
+        stacked.append(jnp.concatenate([twice, once], axis=0))
+    total = dot_nt(jnp.concatenate(spread, axis=1), jnp.concatenate(stacked, axis=1))
+    total = fold(total, rank)
     sent = lanes(dot(triple_left(total), rise).astype(BF16))
     for j in range(group_ref.shape[0]):
         group_ref[j] = sent
@@ -145,7 +149,7 @@
 
 
 def path_kernel(
-    kind_hbm, table_hbm, parent_hbm, transfer_hbm, z_ref, yx_ref, fall_ref, far_ref, spread_ref,
+    kind_hbm, table_hbm, parent_hbm, transfer_hbm, z_ref, yx_ref, far_ref, spread_ref,
     kind_ref, table_ref, parent_ref, transfer_ref, arrived,
 ):
     for copy in bring(
@@ -166,7 +170,9 @@
         z_ref[j, :, 2 * rank :] = jnp.concatenate(halves(block), axis=1)
 
     y_trees, fall = path_blocks(g, groups, 0, low, None, *tree, False)
-    fall_ref[...] = jnp.concatenate(halves(fall), axis=1)
+    both = jnp.concatenate(halves(fall), axis=1)
+    for y in range(1 << Y_BITS):
+        yx_ref[(1 << (X_BITS + Y_BITS)) + y] = both
     down = dot(triple_left(inner), triple_right(fall))
     x_trees, _ = path_blocks(g, groups, high, high + X_BITS, down, *tree, False)
     here = g >> high
@@ -183,16 +189,16 @@
         far_ref[kind, :rank, :] = jnp.concatenate([above, above], axis=1)
         far_ref[kind, rank:, :] = jnp.concatenate([below, jnp.zeros_like(below)], axis=1)
     for i in range(transfer_ref.shape[0]):
-        spread_ref[i] = triple_right(transfer_ref[i])
+        spread_ref[:, i * rank : (i + 1) * rank] = triple_right(transfer_ref[i])
 
 
 def middle_kernel(seen_ref, z_ref, own_ref, sent_ref):
     count = seen_ref.shape[0]
     rank = z_ref.shape[1]
     rows = own_ref.shape[0]
-    total = dot(unlanes(seen_ref[0]), z_ref[0])
-    for j in range(1, count):
-        total += dot(unlanes(seen_ref[j]), z_ref[j])
+    total = dot(
+        unlanes([seen_ref[j] for j in range(count)]), z_ref[...].reshape(count * rank, 4 * rank)
+    )
     inside = lanes(fold(total[:, : 2 * rank], rank).astype(BF16))
     outside = lanes(fold(total[:, 2 * rank :], rank).astype(BF16))
     own = own_ref[...]
@@ -263,20 +269,18 @@
         out_ref[:, i * rows : (i + 1) * rows] = total
 
 
-def last_kernel(seen_ref, yx_ref, fall_ref, spread_ref, local_ref, basis_ref, out_ref):
+def last_kernel(seen_ref, yx_ref, spread_ref, local_ref, basis_ref, out_ref):
     count, rows, _ = seen_ref.shape
     leaves, rank, width = basis_ref.shape
     half = rows // 2
     start = (lax.axis_index("leaf") >> (Y_BITS + Z_BITS)) << Y_BITS
-    total = dot(unlanes(seen_ref[0, :half]), yx_ref[0])
-    for j in range(1, count):
-        total += dot(unlanes(seen_ref[j, :half]), yx_ref[j])
-    for y in range(1 << Y_BITS):
-        total += dot(unlanes(seen_ref[start + y, half:]), fall_ref[...])
+    parts = [seen_ref[j, :half] for j in range(count)]
+    parts += [seen_ref[start + y, half:] for y in range(1 << Y_BITS)]
+    total = dot(unlanes(parts), yx_ref[...].reshape(len(parts) * rank, 2 * rank))
     group = triple_left(fold(total, rank))
+    fields = (dot(group, spread_ref[...]) + local_ref[:, leaves * width :]).astype(BF16)
     for i in range(leaves):
-        far = local_ref[:, leaves * width + i * rank : leaves * width + (i + 1) * rank]
-        field = (dot(group, spread_ref[i]) + far).astype(BF16)
+        field = fields[:, i * rank : (i + 1) * rank]
         at = slice(i * width, (i + 1) * width)
         out_ref[:, at] = (local_ref[:, at] + dot(field, basis_ref[i])).astype(BF16)
 
@@ -347,14 +351,13 @@
     before = lax.ppermute(packed, "leaf", up)
     after = lax.ppermute(packed, "leaf", [(b, a) for a, b in up])
     other_blocks = lax.ppermute(near_blocks, "cols", [(0, 1), (1, 0)])
-    z_table, yx_table, fall, far_table, spread = call(
+    z_table, yx_table, far_table, spread = call(
         path_kernel,
         (
             shape((size, rank, 4 * rank), BF16),
-            shape((across, rank, 2 * rank), BF16),
-            shape((rank, 2 * rank), BF16),
+            shape((across + (1 << Y_BITS), rank, 2 * rank), BF16),
             shape((kinds, 2 * rank, 2 * rank), BF16),
-            shape((leaves, 3 * rank, rank), BF16),
+            shape((3 * rank, leaves * rank), BF16),
         ),
         [hbm] * 4, 2**28, 2**20, 8,
         [
@@ -384,8 +387,8 @@
         before, packed, after, blocks_here, stay(other_blocks)[0], far_table,
     )
     return call(
-        last_kernel, shape((cols, width), BF16), [vm] * 6, 2**27, 2**21, 8
-    )(seen_yx, yx_table, fall, spread, local, cluster_basis)
+        last_kernel, shape((cols, width), BF16), [vm] * 5, 2**27, 2**21, 8
+    )(seen_yx, yx_table, spread, local, cluster_basis)
 
 
 def solution(mesh):

time: 53.9 us -> 52.8 us (0.980)
  Pallas kernels: 15.5 us -> 14.4 us
    pallas_call x2, Pallas kernels: 5.65 us -> 4.8 us  [the longest x1 3.33 us: shards(): call(path_kernel, (shape((size, rank, 4 * rank), BF16), shape((across + (...]
where the time goes in v2:
time: 52.8 us; the launch traced here: 52.4 us
  starting transfers between devices  30.5 us (58%)
  Pallas kernels  14.4 us (27%)
  waiting for transfers between devices  7.34 us (14%)
    all_to_all x1, starting transfers between devices, shards(): lax.all_to_all(group, 'leaf', 0, 0, axis_index_groups=z_groups, tiled=True)  15.2 us
    all_to_all x1, starting transfers between devices, shards(): lax.all_to_all(sent, 'leaf', 0, 0, axis_index_groups=yx_groups, tiled=True)  7.03 us
    pallas_call x1, Pallas kernels, shards(): call(near_kernel, shape((cols, width + leaves * rank), F32), [hbm] * 3 +...  5.84 us
    all_to_all x1, waiting for transfers between devices, shards(): lax.all_to_all(group, 'leaf', 0, 0, axis_index_groups=z_groups, tiled=True)  4.75 us
    ppermute x1, starting transfers between devices, shards(): after = lax.ppermute(packed, 'leaf', [(b, a) for a, b in up])  4.45 us
    pallas_call x1, Pallas kernels, shards(): call(path_kernel, (shape((size, rank, 4 * rank), BF16), shape((across + (...  3.33 us
    pallas_call x1, Pallas kernels, shards(): call(coef_kernel, (shape((cols, packed_width), BF16), shape((size, *own_l...  2.66 us
    all_to_all x1, waiting for transfers between devices, shards(): lax.all_to_all(sent, 'leaf', 0, 0, axis_index_groups=yx_groups, tiled=True)  2.58 us
  transfers between devices with their start and end apart: 5, of which 2 were waited for; matrix products, arithmetic and copies ran while one was open for 0% of the time, Pallas kernels for 25%

profile of v2, /device:TPU:32, one launch (start us, length us, event | category | flops | bytes accessed | tf_op | source)
XLA Modules:
  0.0 52.4 jit_solution(12778649672787004730)
XLA Ops:
  0.0 1.9 %collective-permute-start.2 = (bf16[8,8,128,256]{3,2,1,0:T(8,128)(2,1)}, bf16[8,8,128,256]{3,2,1,0:T(8,128)(2,1)}, u32[]{:S(2)}, u32[]{:S(2)}) collective-permute-start(bf16[8,8,128,256]{3,2,1,0:T(8,128)(2,1)} %own_ref.1), channel_id=1, source_target_pairs={{0,1},{1,0},{2,3},{3,2},{4,5},{5,4},{6,7},{7,6},{8,9},{9,8},{10,11... | collective-permute-start | bytes 12582920 | tf_op jit(solution)/shard_map/ppermute | solution.py:353
  1.9 2.7 %shard_map.100 = (bf16[64,3072]{1,0:T(8,128)(2,1)S(1)}, bf16[16,32,128]{2,1,0:T(8,128)(2,1)}, bf16[32,128]{1,0:T(8,128)(2,1)S(1)}) custom-call(bf16[64,2048]{1,0:T(8,128)(2,1)} %x_hbm.1, bf16[8,64,256]{2,1,0:T(8,128)(2,1)} %basis_ref.1, f32[8,64,64]{2,1,0:T(8,128)} %transfer_hbm.3, f32[2,64,64]{2,1,0:T(8,128)} %parent_hbm.3), custom_call_target="tpu_custom_call" | custom-call | flops 67108864 | bytes 1048576 | tf_op jit(solution)/shard_map/pallas_call | solution.py:337
  4.6 15.2 %all-to-all-start = ((bf16[16,32,128]{2,1,0:T(8,128)(2,1)}), bf16[16,32,128]{2,1,0:T(8,128)(2,1)S(1)}, u32[]{:S(2)}, u32[]{:S(2)}) async-start(bf16[16,32,128]{2,1,0:T(8,128)(2,1)} %get-tuple-element.12), calls=%async_computation | async-start | bytes 262144 | tf_op jit(solution)/shard_map/all_to_all | solution.py:350
  19.8 4.5 %collective-permute-start.1 = (bf16[64,3072]{1,0:T(8,128)(2,1)S(1)}, bf16[64,3072]{1,0:T(8,128)(2,1)S(1)}, u32[]{:S(2)}, u32[]{:S(2)}) collective-permute-start(bf16[64,3072]{1,0:T(8,128)(2,1)S(1)} %get-tuple-element.17.packed_ref), channel_id=1, source_target_pairs={{2,0},{4,2},{6,4},{8,6},{10,8},{12,10},{14,12},{16,14},{18,16},{20... | collective-permute-start | bytes 1179656 | tf_op jit(solution)/shard_map/ppermute | solution.py:352
  24.3 1.9 %collective-permute-start = (bf16[64,3072]{1,0:T(8,128)(2,1)S(1)}, bf16[64,3072]{1,0:T(8,128)(2,1)S(1)}, u32[]{:S(2)}, u32[]{:S(2)}) collective-permute-start(bf16[64,3072]{1,0:T(8,128)(2,1)S(1)} %get-tuple-element.17.packed_ref), channel_id=1, source_target_pairs={{0,2},{2,4},{4,6},{6,8},{8,10},{10,12},{12,14},{14,16},{16,18},{18... | collective-permute-start | bytes 1179656 | tf_op jit(solution)/shard_map/ppermute | solution.py:351
  26.2 3.3 %shard_map.101 = (bf16[16,64,256]{2,1,0:T(8,128)(2,1)S(1)}, bf16[20,64,128]{2,1,0:T(8,128)(2,1)S(1)}, bf16[16,128,128]{2,1,0:T(8,128)(2,1)S(1)}, bf16[192,512]{1,0:T(8,128)(2,1)S(1)}) custom-call(s32[255]{0:T(256)} %kind_hbm.1, f32[16,64,64]{2,1,0:T(8,128)} %table_hbm.1, f32[2,64,64]{2,1,0:T(8,128)} %parent_hbm.3, f32[8,64,64]{2,1,0:T(8,128)} %transfer_hbm.3), custom_call_target="tpu_custom_call" | custom-call | flops 268435456 | bytes 1048576 | tf_op jit(solution)/shard_map/pallas_call | solution.py:354
  29.5 4.8 %all-to-all-done.seen_ref = bf16[16,32,128]{2,1,0:T(8,128)(2,1)S(1)} async-done(((bf16[16,32,128]{2,1,0:T(8,128)(2,1)}), bf16[16,32,128]{2,1,0:T(8,128)(2,1)S(1)}, u32[]{:S(2)}, u32[]{:S(2)}) %all-to-all-start) | async-done | bytes 131104 | tf_op jit(solution)/shard_map/all_to_all | solution.py:350
  34.3 1.1 %shard_map.102 = bf16[16,64,128]{2,1,0:T(8,128)(2,1)} custom-call(bf16[16,32,128]{2,1,0:T(8,128)(2,1)S(1)} %all-to-all-done.seen_ref, bf16[16,64,256]{2,1,0:T(8,128)(2,1)S(1)} %get-tuple-element.13.z_ref, bf16[32,128]{1,0:T(8,128)(2,1)S(1)} %get-tuple-element.14.own_ref), custom_call_target="tpu_custom_call" | custom-call | flops 33554432 | bytes 524288 | tf_op jit(solution)/shard_map/pallas_call | solution.py:368
  35.4 7.0 %all-to-all-start.1 = ((bf16[16,64,128]{2,1,0:T(8,128)(2,1)}), bf16[16,64,128]{2,1,0:T(8,128)(2,1)S(1)}, u32[]{:S(2)}, u32[]{:S(2)}) async-start(bf16[16,64,128]{2,1,0:T(8,128)(2,1)} %shard_map.102), calls=%async_computation.1 | async-start | bytes 524288 | tf_op jit(solution)/shard_map/all_to_all | solution.py:372
  42.4 0.0 collective-permute-done.1.after_ref
  42.5 0.0 collective-permute-done.before_ref
  42.5 0.0 collective-permute-done.2.other_ref
  42.5 0.0 copy-start
  42.5 5.8 %shard_map.103.local_ref = f32[64,2560]{1,0:T(8,128)S(1)} custom-call(s32[8,8]{1,0:T(8,128)} %near_hbm.1, s32[8,8]{1,0:T(8,128)} %far_index_hbm.1, s32[8,8]{1,0:T(8,128)} %far_kind_hbm.1, bf16[64,3072]{1,0:T(8,128)(2,1)S(1)} %collective-permute-done.before_ref, bf16[64,3072]{1,0:T(8,128)(2,1)S(1)} %get-tuple-element.17.packed_ref, ...), custom_call_target="tpu_custom_call" | custom-call | flops 1073741824 | bytes 10485760 | tf_op jit(solution)/shard_map/pallas_call | solution.py:373
  48.3 2.6 %all-to-all-done.1.seen_ref = bf16[16,64,128]{2,1,0:T(8,128)(2,1)S(1)} async-done(((bf16[16,64,128]{2,1,0:T(8,128)(2,1)}), bf16[16,64,128]{2,1,0:T(8,128)(2,1)S(1)}, u32[]{:S(2)}, u32[]{:S(2)}) %all-to-all-start.1) | async-done | bytes 262176 | tf_op jit(solution)/shard_map/all_to_all | solution.py:372
  50.9 0.0 copy-done
  50.9 1.5 %shard_map.104 = bf16[64,2048]{1,0:T(8,128)(2,1)} custom-call(bf16[16,64,128]{2,1,0:T(8,128)(2,1)S(1)} %all-to-all-done.1.seen_ref, bf16[20,64,128]{2,1,0:T(8,128)(2,1)S(1)} %get-tuple-element.15.yx_ref, bf16[192,512]{1,0:T(8,128)(2,1)S(1)} %get-tuple-element.16.spread_ref, f32[64,2560]{1,0:T(8,128)S(1)} %shard_map.103.local_ref, bf16[8,64,256]{2,1,0:T(8,128)(2,1)S(1)} %copy-done), custom_call_target="tpu_custom_call" | custom-call | flops 134217728 | bytes 2097152 | tf_op jit(solution)/shard_map/pallas_call | solution.py:389
Async XLA Ops:
  0.0 42.5 %collective-permute-start.2 = (bf16[8,8,128,256]{3,2,1,0:T(8,128)(2,1)}, bf16[8,8,128,256]{3,2,1,0:T(8,128)(2,1)}, u32[]{:S(2)}, u32[]{:S(2)}) collective-permute-start(bf16[8,8,128,256]{3,2,1,0:T(8,128)(2,1)} %own_ref.1), channel_id=1, source_target_pairs={{0,1},{1,0},{2,3},{3,2},{4,5},{5,4},{6,7},{7,6},{8,9},{9,8},{10,11... | collective-permute-start | bytes 12582920 | tf_op jit(solution)/shard_map/ppermute | solution.py:353
  4.6 29.7 %all-to-all-start = ((bf16[16,32,128]{2,1,0:T(8,128)(2,1)}), bf16[16,32,128]{2,1,0:T(8,128)(2,1)S(1)}, u32[]{:S(2)}, u32[]{:S(2)}) async-start(bf16[16,32,128]{2,1,0:T(8,128)(2,1)} %get-tuple-element.12), calls=%async_computation | async-start | bytes 262144 | tf_op jit(solution)/shard_map/all_to_all | solution.py:350
  19.8 22.6 %collective-permute-start.1 = (bf16[64,3072]{1,0:T(8,128)(2,1)S(1)}, bf16[64,3072]{1,0:T(8,128)(2,1)S(1)}, u32[]{:S(2)}, u32[]{:S(2)}) collective-permute-start(bf16[64,3072]{1,0:T(8,128)(2,1)S(1)} %get-tuple-element.17.packed_ref), channel_id=1, source_target_pairs={{2,0},{4,2},{6,4},{8,6},{10,8},{12,10},{14,12},{16,14},{18,16},{20... | collective-permute-start | bytes 1179656 | tf_op jit(solution)/shard_map/ppermute | solution.py:352
  24.3 18.2 %collective-permute-start = (bf16[64,3072]{1,0:T(8,128)(2,1)S(1)}, bf16[64,3072]{1,0:T(8,128)(2,1)S(1)}, u32[]{:S(2)}, u32[]{:S(2)}) collective-permute-start(bf16[64,3072]{1,0:T(8,128)(2,1)S(1)} %get-tuple-element.17.packed_ref), channel_id=1, source_target_pairs={{0,2},{2,4},{4,6},{6,8},{8,10},{10,12},{12,14},{14,16},{16,18},{18... | collective-permute-start | bytes 1179656 | tf_op jit(solution)/shard_map/ppermute | solution.py:351
  35.4 15.5 %all-to-all-start.1 = ((bf16[16,64,128]{2,1,0:T(8,128)(2,1)}), bf16[16,64,128]{2,1,0:T(8,128)(2,1)S(1)}, u32[]{:S(2)}, u32[]{:S(2)}) async-start(bf16[16,64,128]{2,1,0:T(8,128)(2,1)} %shard_map.102), calls=%async_computation.1 | async-start | bytes 524288 | tf_op jit(solution)/shard_map/all_to_all | solution.py:372
  42.5 8.4 %copy-start = (bf16[8,64,256]{2,1,0:T(8,128)(2,1)S(1)}, bf16[8,64,256]{2,1,0:T(8,128)(2,1)}, u32[]{:S(2)}) copy-start(bf16[8,64,256]{2,1,0:T(8,128)(2,1)} %basis_ref.1) | copy-start | bytes 786436
